TPU v7x, 32 devices: a whole 2x2x4 slice. The times are simulated.
32 devices in a mesh: dp: 8 (over z, y), tensor: 4 (over x, core).
Axes of the slice: x: 2, y: 2, z: 4, core: 2. Of those that a mesh axis runs over, the one named last changes fastest.
Arguments:
- tokens: bfloat16 [2048, 2048], P('dp'), may hold values from -6 to 6
- documents: int32 [8, 256], P('dp'), may hold values from 0 to 7, never falling along the last dimension, each value on 1 to 128 neighbouring positions
- cotangent: bfloat16 [2048, 2048], P('dp'), may hold values from -6 to 6
- qkv_weight: float32 [3, 2048, 2048], P(None, 'dp', 'tensor'), may hold values from -0.1875 to 0.1875
- out_weight: float32 [2048, 2048], P(('tensor', 'dp')), may hold values from -0.25 to 0.25
- lift_weight: float32 [2, 2048, 8192], P(None, 'dp', 'tensor'), may hold values from -0.125 to 0.125
- down_weight: float32 [8192, 2048], P(('tensor', 'dp')), may hold values from -0.0625 to 0.0625
- gains: float32 [2, 2048], P(None, 'dp'), may hold values from 0.5 to 1.5
- qkv_first: float32 [3, 2048, 2048], P(None, 'dp', 'tensor'), may hold values from -3.5 to 3.5
- out_first: float32 [2048, 2048], P(('tensor', 'dp')), may hold values from -3.5 to 3.5
- lift_first: float32 [2, 2048, 8192], P(None, 'dp', 'tensor'), may hold values from -3.5 to 3.5
- down_first: float32 [8192, 2048], P(('tensor', 'dp')), may hold values from -3.5 to 3.5
- gains_first: float32 [2, 2048], P(None, 'dp'), may hold values from -3.5 to 3.5
- qkv_second: float32 [3, 2048, 2048], P(None, 'dp', 'tensor'), may hold values from 0.21038716 to 0.8415486
- out_second: float32 [2048, 2048], P(('tensor', 'dp')), may hold values from 0.21038716 to 0.8415486
- lift_second: float32 [2, 2048, 8192], P(None, 'dp', 'tensor'), may hold values from 0.21038716 to 0.8415486
- down_second: float32 [8192, 2048], P(('tensor', 'dp')), may hold values from 0.21038716 to 0.8415486
- gains_second: float32 [2, 2048], P(None, 'dp'), may hold values from 0.21038716 to 0.8415486
Outputs:
- layer_out: bfloat16 [2048, 2048], P('dp')
- grad_tokens: float32 [2048, 2048], P('dp')
- qkv_new: float32 [3, 2048, 2048], P(None, 'dp', 'tensor')
- out_new: float32 [2048, 2048], P(('tensor', 'dp'))
- lift_new: float32 [2, 2048, 8192], P(None, 'dp', 'tensor')
- down_new: float32 [8192, 2048], P(('tensor', 'dp'))
- gains_new: float32 [2, 2048], P(None, 'dp')
- qkv_moment: float32 [3, 2048, 2048], P(None, 'dp', 'tensor')
- out_moment: float32 [2048, 2048], P(('tensor', 'dp'))
- lift_moment: float32 [2, 2048, 8192], P(None, 'dp', 'tensor')
- down_moment: float32 [8192, 2048], P(('tensor', 'dp'))
- gains_moment: float32 [2, 2048], P(None, 'dp')
- qkv_variance: float32 [3, 2048, 2048], P(None, 'dp', 'tensor')
- out_variance: float32 [2048, 2048], P(('tensor', 'dp'))
- lift_variance: float32 [2, 2048, 8192], P(None, 'dp', 'tensor')
- down_variance: float32 [8192, 2048], P(('tensor', 'dp'))
- gains_variance: float32 [2, 2048], P(None, 'dp')
- grad_norm: float32 [], replicated
Inputs may be any that keep to these rules, and one draw needn't show every extreme that they name: Each row of documents is one sequence: ids never fall along the row, and each id is one document of 1 to 128 tokens.
All inputs are finite; a program needn't handle non-finite values.
Results may differ from a plain program's by a relative error of at most 0.015.
The roundings to bfloat16 on the way count: a program that leaves them out, or rounds other values in their place, can miss the bound.
Values may be sent and summed in bfloat16 or wider, within the bound.
No kernel may reach another device: no remote copies, remote signals or barrier semaphores. Data moves between devices by JAX's collectives and lax.ppermute only.
A program may use at most 256 MiB of HBM per device.

v0:
```python
import math
import jax
import jax.numpy as jnp
from jax import lax
from jax.sharding import PartitionSpec as P

HD = 128
STEP = 10
CLIP_NORM = 16384
norm_eps = 1e-05
beta_one = 0.9
beta_two = 0.95
adam_eps = 1e-08
rate_matrix = 0.02
rate_gain = 0.5
decay_matrix = 0.1


def norm_forward(rows, gain):
    inverse = lax.rsqrt(jnp.mean(rows * rows, axis=-1, keepdims=True) + norm_eps)
    scaled = rows * inverse
    return (scaled, inverse, (scaled * gain).astype(jnp.bfloat16))


def norm_backward(incoming, scaled, inverse, gain):
    grad_gain = jnp.sum(incoming * scaled, axis=0)
    weighted = incoming * gain
    grad_rows = inverse * (weighted - scaled * jnp.mean(weighted * scaled, axis=-1, keepdims=True))
    return (grad_gain, grad_rows)


def block_probs(queries, keys, doc_row, start, block, scale, offset):
    length = keys.shape[0]
    query_pos = start + jnp.arange(block, dtype=jnp.int32)
    key_pos = jnp.arange(length, dtype=jnp.int32)
    allowed = (query_pos[:, None] >= key_pos[None, :]) & (doc_row[:, None] == doc_row[None, :])
    scores = (
        jnp.einsum("qhd,khd->hqk", queries, keys, preferred_element_type=jnp.float32) * scale
        + offset
    )
    probs = jnp.where(allowed[None], jax.nn.sigmoid(scores), 0.0)
    return (queries, probs)


def adam_step(weight, first, second, grad, factor, rate, decay):
    clipped = grad * factor
    moment = beta_one * first + (1.0 - beta_one) * clipped
    variance = beta_two * second + (1.0 - beta_two) * clipped * clipped
    corr_one = 1.0 - beta_one**STEP
    corr_two = 1.0 - beta_two**STEP
    update = moment / corr_one / (jnp.sqrt(variance / corr_two) + adam_eps)
    return (weight - rate * (update + decay * weight), moment, variance)


def on_device(
    tokens,
    documents,
    cotangent,
    qkv_weight,
    out_weight,
    lift_weight,
    down_weight,
    gains,
    qkv_first,
    out_first,
    lift_first,
    down_first,
    gains_first,
    qkv_second,
    out_second,
    lift_second,
    down_second,
    gains_second,
):
    bf16 = jnp.bfloat16
    f32 = jnp.float32
    w_qkv, w_out, w_lift, w_down, w_gains = (
        lax.all_gather(qkv_weight.astype(bf16), "dp", axis=1, tiled=True),
        lax.all_gather(out_weight.astype(bf16), "dp", axis=0, tiled=True),
        lax.all_gather(lift_weight.astype(bf16), "dp", axis=1, tiled=True),
        lax.all_gather(down_weight.astype(bf16), "dp", axis=0, tiled=True),
        lax.all_gather(gains.astype(bf16), "dp", axis=1, tiled=True),
    )
    length = tokens.shape[0]
    local_width = w_qkv.shape[2]
    heads = local_width // HD
    block = min(512, length)
    blocks = length // block
    scale = 1.0 / math.sqrt(HD)
    offset = -math.log(length)
    doc_row = documents[0]
    gain_one = w_gains[0].astype(f32)
    gain_two = w_gains[1].astype(f32)
    x_rows = tokens.astype(f32)
    scaled_one, inverse_one, normed_one = norm_forward(x_rows, gain_one)
    project = jnp.einsum("td,cde->cte", normed_one, w_qkv, preferred_element_type=f32).astype(bf16)
    queries = project[0].reshape(length, heads, HD)
    keys = project[1].reshape(length, heads, HD)
    values = project[2].reshape(length, heads, HD)

    def attend(index):
        start = index * block
        query_block, probs = block_probs(queries, keys, doc_row, start, block, scale, offset)
        return jnp.einsum(
            "hqk,khd->qhd", probs.astype(bf16), values, preferred_element_type=f32
        ).astype(bf16)

    attended = lax.map(attend, jnp.arange(blocks, dtype=jnp.int32)).reshape(length, local_width)
    branch = lax.psum(jnp.dot(attended, w_out, preferred_element_type=f32), "tensor")
    middle = x_rows + branch
    scaled_two, inverse_two, normed_two = norm_forward(middle, gain_two)
    gate_up = jnp.einsum("td,cde->cte", normed_two, w_lift, preferred_element_type=f32)
    gate = gate_up[0]
    upward = gate_up[1]
    sigma = jax.nn.sigmoid(gate)
    hidden = (gate * sigma * upward).astype(bf16)
    feed = lax.psum(
        jnp.dot(hidden, w_down, preferred_element_type=f32).astype(jnp.bfloat16), "tensor"
    ).astype(jnp.float32)
    layer_out = (middle + feed).astype(bf16)
    grad_incoming = cotangent.astype(f32)
    grad_down = jnp.einsum("tf,td->fd", hidden, cotangent, preferred_element_type=f32)
    grad_hidden = jnp.einsum("td,fd->tf", cotangent, w_down, preferred_element_type=f32)
    grad_gate = (grad_hidden * upward * sigma * (1.0 + gate * (1.0 - sigma))).astype(bf16)
    grad_up = (grad_hidden * gate * sigma).astype(bf16)
    grad_pair = jnp.stack([grad_gate, grad_up])
    grad_lift = jnp.einsum("td,ctf->cdf", normed_two, grad_pair, preferred_element_type=f32)
    back_two = lax.psum(
        jnp.einsum("ctf,cdf->td", grad_pair, w_lift, preferred_element_type=f32), "tensor"
    )
    grad_gain_two, grad_mid_norm = norm_backward(back_two, scaled_two, inverse_two, gain_two)
    grad_mid = grad_incoming + grad_mid_norm
    grad_branch = grad_mid.astype(bf16)
    grad_out = jnp.einsum("te,td->ed", attended, grad_branch, preferred_element_type=f32)
    grad_attended = jnp.einsum("td,ed->te", grad_branch, w_out, preferred_element_type=f32).astype(
        bf16
    )
    grad_heads = grad_attended.reshape(length, heads, HD)

    def attend_back(carry, index):
        grad_keys, grad_values = carry
        start = index * block
        query_block, probs = block_probs(queries, keys, doc_row, start, block, scale, offset)
        grad_probs = jnp.einsum("qhd,khd->hqk", grad_heads, values, preferred_element_type=f32)
        grad_scores = (grad_probs * probs * (1.0 - probs)).astype(bf16)
        grad_query = (
            jnp.einsum("hqk,khd->qhd", grad_scores, keys, preferred_element_type=f32) * scale
        )
        grad_keys = (
            grad_keys
            + jnp.einsum("hqk,qhd->khd", grad_scores, query_block, preferred_element_type=f32)
            * scale
        )
        grad_values = grad_values + jnp.einsum(
            "hqk,qhd->khd", probs.astype(bf16), grad_heads, preferred_element_type=f32
        )
        return ((grad_keys, grad_values), grad_query)

    zeros_kv = jnp.zeros((length, heads, HD), f32)
    (grad_keys, grad_values), grad_queries = lax.scan(
        attend_back, (zeros_kv, zeros_kv), jnp.arange(blocks, dtype=jnp.int32)
    )
    grad_project = jnp.stack(
        [
            grad_queries.reshape(length, local_width),
            grad_keys.reshape(length, local_width),
            grad_values.reshape(length, local_width),
        ]
    ).astype(bf16)
    grad_qkv = jnp.einsum("td,cte->cde", normed_one, grad_project, preferred_element_type=f32)
    back_one = lax.psum(
        jnp.einsum("cte,cde->td", grad_project, w_qkv, preferred_element_type=f32), "tensor"
    )
    grad_gain_one, grad_x_norm = norm_backward(back_one, scaled_one, inverse_one, gain_one)
    grad_tokens = grad_mid + grad_x_norm
    grad_gains = jnp.stack([grad_gain_one, grad_gain_two])
    red_qkv, red_out, red_lift, red_down, red_gains = (
        lax.psum_scatter(grad_qkv, "dp", scatter_dimension=1, tiled=True),
        lax.psum_scatter(grad_out, "dp", scatter_dimension=0, tiled=True),
        lax.psum_scatter(grad_lift, "dp", scatter_dimension=1, tiled=True),
        lax.psum_scatter(grad_down, "dp", scatter_dimension=0, tiled=True),
        lax.psum_scatter(grad_gains, "dp", scatter_dimension=1, tiled=True),
    )
    local_total = (
        jnp.sum(red_qkv * red_qkv)
        + jnp.sum(red_out * red_out)
        + jnp.sum(red_lift * red_lift)
        + jnp.sum(red_down * red_down)
        + jnp.sum(red_gains * red_gains) / lax.axis_size("tensor")
    )
    total = lax.psum(local_total, ("dp", "tensor"))
    grad_norm = jnp.sqrt(total)
    factor = CLIP_NORM / jnp.maximum(grad_norm, CLIP_NORM)
    qkv_new, qkv_moment, qkv_variance = adam_step(
        qkv_weight, qkv_first, qkv_second, red_qkv, factor, rate_matrix, decay_matrix
    )
    out_new, out_moment, out_variance = adam_step(
        out_weight, out_first, out_second, red_out, factor, rate_matrix, decay_matrix
    )
    lift_new, lift_moment, lift_variance = adam_step(
        lift_weight, lift_first, lift_second, red_lift, factor, rate_matrix, decay_matrix
    )
    down_new, down_moment, down_variance = adam_step(
        down_weight, down_first, down_second, red_down, factor, rate_matrix, decay_matrix
    )
    gains_new, gains_moment, gains_variance = adam_step(
        gains, gains_first, gains_second, red_gains, factor, rate_gain, 0.0
    )
    return (
        layer_out,
        grad_tokens,
        qkv_new,
        out_new,
        lift_new,
        down_new,
        gains_new,
        qkv_moment,
        out_moment,
        lift_moment,
        down_moment,
        gains_moment,
        qkv_variance,
        out_variance,
        lift_variance,
        down_variance,
        gains_variance,
        grad_norm,
    )


def solution(mesh):
    placed = (
        P("dp", None),
        P("dp", None),
        P("dp", None),
        P(None, "dp", "tensor"),
        P(("tensor", "dp"), None),
        P(None, "dp", "tensor"),
        P(("tensor", "dp"), None),
        P(None, "dp"),
        P(None, "dp", "tensor"),
        P(("tensor", "dp"), None),
        P(None, "dp", "tensor"),
        P(("tensor", "dp"), None),
        P(None, "dp"),
        P(None, "dp", "tensor"),
        P(("tensor", "dp"), None),
        P(None, "dp", "tensor"),
        P(("tensor", "dp"), None),
        P(None, "dp"),
    )
    return jax.shard_map(
        on_device,
        mesh=mesh,
        in_specs=placed,
        out_specs=(
            P("dp", None),
            P("dp", None),
            P(None, "dp", "tensor"),
            P(("tensor", "dp"), None),
            P(None, "dp", "tensor"),
            P(("tensor", "dp"), None),
            P(None, "dp"),
            P(None, "dp", "tensor"),
            P(("tensor", "dp"), None),
            P(None, "dp", "tensor"),
            P(("tensor", "dp"), None),
            P(None, "dp"),
            P(None, "dp", "tensor"),
            P(("tensor", "dp"), None),
            P(None, "dp", "tensor"),
            P(("tensor", "dp"), None),
            P(None, "dp"),
            P(),
        ),
        check_vma=False,
    )
```

profile of v0, /device:TPU:0, one launch (start us, length us, event | category | flops | bytes accessed | tf_op | source)
XLA Modules:
  0.0 2062.5 jit_solution(4781406800349877402)
XLA Ops:
  10.7 22.7 %all_gather.15 = bf16[2,2048]{1,0:T(2,128)(2,1)S(1)} all-gather(bf16[2,256]{1,0:T(2,128)(2,1)S(1)} %convert_element_type.80), channel_id=1, replica_groups=mesh['dp'=8,'tensor'=4] {'dp'}, dimensions={1}, use_global_device_ids=true | all-gather | bytes 9216 | tf_op jit(solution)/shard_map/all_gather | solution.py:82
  33.8 78.4 %all-gather.5.cloned.1.call-done = bf16[3,2048,512]{2,1,0:T(8,128)(2,1)} async-done(((bf16[3,256,512]{2,1,0:T(8,128)(2,1)}), bf16[3,2048,512]{2,1,0:T(8,128)(2,1)}) %all-gather.5.cloned.1.call-update) | async-done | bytes 6291472 | tf_op jit(solution)/shard_map/all_gather | solution.py:78
  112.3 4.6 fusion.22
  119.3 43.0 %all-gather.7.cloned.1.call-done = bf16[512,2048]{1,0:T(8,128)(2,1)} async-done(((bf16[64,2048]{1,0:T(8,128)(2,1)}), bf16[512,2048]{1,0:T(8,128)(2,1)}) %all-gather.7.cloned.1.call-update) | async-done | bytes 2097168 | tf_op jit(solution)/shard_map/all_gather | solution.py:79
  173.0 43.1 %all-reduce.5.cloned.1.call-done = f32[256,2048]{1,0:T(8,128)} async-done(((f32[256,2048]{1,0:T(8,128)}), f32[256,2048]{1,0:T(8,128)}) %all-reduce.5.cloned.1.call-update) | async-done | bytes 2097168 | tf_op jit(solution)/shard_map/psum | solution.py:109
  218.0 228.0 %all-gather.9.cloned.1.call-done = bf16[2,2048,2048]{2,1,0:T(8,128)(2,1)} async-done(((bf16[2,256,2048]{2,1,0:T(8,128)(2,1)}), bf16[2,2048,2048]{2,1,0:T(8,128)(2,1)}) %all-gather.9.cloned.1.call-update) | async-done | bytes 16777232 | tf_op jit(solution)/shard_map/all_gather | solution.py:80
  446.0 10.2 convolution_bitcast_fusion.2
  456.3 115.0 %all-gather.11.cloned.1.call-done = bf16[2048,2048]{1,0:T(8,128)(2,1)} async-done(((bf16[256,2048]{1,0:T(8,128)(2,1)}), bf16[2048,2048]{1,0:T(8,128)(2,1)}) %all-gather.11.cloned.1.call-update) | async-done | bytes 8388624 | tf_op jit(solution)/shard_map/all_gather | solution.py:81
  571.3 9.7 fusion.28
  580.9 12.3 convolution_bitcast_fusion.4
  593.3 7.1 convolution_convert_fusion
  600.9 42.0 %all-reduce.9.cloned.1.call-done = f32[256,2048]{1,0:T(8,128)} async-done(((f32[256,2048]{1,0:T(8,128)}), f32[256,2048]{1,0:T(8,128)}) %all-reduce.9.cloned.1.call-update) | async-done | bytes 2097168 | tf_op jit(solution)/shard_map/psum | solution.py:128
  645.1 37.2 %all-reduce.7.cloned.1.call-done = bf16[256,2048]{1,0:T(8,128)(2,1)} async-done(((bf16[256,2048]{1,0:T(8,128)(2,1)}), bf16[256,2048]{1,0:T(8,128)(2,1)}) %all-reduce.7.cloned.1.call-update) | async-done | bytes 1048592 | tf_op jit(solution)/shard_map/psum | solution.py:117
  701.9 6.2 convolution_bitcast_fusion.3
  708.2 52.0 %all-reduce.11.cloned.1.call-done = f32[256,2048]{1,0:T(8,128)} async-done(((f32[256,2048]{1,0:T(8,128)}), f32[256,2048]{1,0:T(8,128)}) %all-reduce.11.cloned.1.call-update) | async-done | bytes 2097168 | tf_op jit(solution)/shard_map/psum | solution.py:171
  769.1 7.5 convolution_bitcast_fusion.1
  776.7 9.7 fusion.54
  786.6 15.0 convolution_bitcast_fusion
  804.6 5.5 copy.83
  814.7 5.4 copy.80
  820.1 5.4 copy.81
  830.7 89.1 %reduce-scatter.10.cloned.1.call-done = f32[64,2048]{1,0:T(8,128)} async-done(((f32[512,2048]{1,0:T(8,128)}), f32[64,2048]{1,0:T(8,128)}) %reduce-scatter.10.cloned.1.call-update) | async-done | bytes 524304 | tf_op jit(solution)/shard_map/reduce_scatter | solution.py:179
  921.6 209.4 %reduce-scatter.8.cloned.1.call-done = f32[3,256,512]{1,2,0:T(8,128)} async-done(((f32[3,2048,512]{1,2,0:T(8,128)}), f32[3,256,512]{1,2,0:T(8,128)}) %reduce-scatter.8.cloned.1.call-update) | async-done | bytes 1572880 | tf_op jit(solution)/shard_map/reduce_scatter | solution.py:178
  1134.7 279.3 %reduce-scatter.14.cloned.1.call-done = f32[256,2048]{1,0:T(8,128)} async-done(((f32[2048,2048]{1,0:T(8,128)}), f32[256,2048]{1,0:T(8,128)}) %reduce-scatter.14.cloned.1.call-update) | async-done | bytes 2097168 | tf_op jit(solution)/shard_map/reduce_scatter | solution.py:181
  1416.7 538.9 %reduce-scatter.12.cloned.1.call-done = f32[2,256,2048]{1,2,0:T(8,128)} async-done(((f32[2,2048,2048]{1,2,0:T(8,128)}), f32[2,256,2048]{1,2,0:T(8,128)}) %reduce-scatter.12.cloned.1.call-update) | async-done | bytes 4194320 | tf_op jit(solution)/shard_map/reduce_scatter | solution.py:180
  1964.2 39.5 %psum.39 = f32[]{:T(128)} all-reduce(f32[]{:T(128)S(6)} %add.183), channel_id=1, replica_groups=mesh['dp'=8,'tensor'=4] {'dp','tensor'}, use_global_device_ids=true, to_apply=%region_20.21 | all-reduce | flops 1 | bytes 8 | tf_op jit(solution)/shard_map/psum | solution.py:191
  2004.4 5.7 multiply_subtract_fusion.2
  2013.1 11.3 multiply_subtract_fusion
  2024.5 5.3 copy.85
  2032.8 5.3 copy.87
  2039.8 5.5 copy.89
  2048.6 6.1 multiply_subtract_fusion.1
  (125 shorter events, 87.9 us)
Async XLA Ops:
  7.2 2.7 copy-start.11
  7.2 3.5 copy-start.20
  7.2 26.2 %copy-start.2 = (bf16[256,2048]{1,0:T(8,128)(2,1)S(1)}, bf16[256,2048]{1,0:T(8,128)(2,1)}, u32[]{:S(2)}) copy-start(bf16[256,2048]{1,0:T(8,128)(2,1)} %param.18) | copy-start | bytes 3145732
  7.2 26.5 %copy-start.21 = (s32[1,256]{1,0:T(1,128)S(1)}, s32[1,256]{1,0:T(1,128)}, u32[]{:S(2)}) copy-start(s32[1,256]{1,0:T(1,128)} %param.19) | copy-start | bytes 3076
  7.2 105.0 %all-gather.5.cloned.1.call-start = ((), (), s32[]{:S(2)}) async-start(), calls=%async_computation.5 | async-start | bytes 7077888 | tf_op jit(solution)/shard_map/all_gather | solution.py:78
  9.8 152.5 %all-gather.7.cloned.1.call-start = ((), (), s32[]{:S(2)}) async-start(), calls=%async_computation.6 | async-start | bytes 2359296 | tf_op jit(solution)/shard_map/all_gather | solution.py:79
  10.6 205.5 %all-reduce.5.cloned.1.call-start = ((), (), s32[]{:S(2)}) async-start(), calls=%async_computation.7 | async-start | bytes 4194304 | tf_op jit(solution)/shard_map/psum | solution.py:109
  166.0 280.1 %all-gather.9.cloned.1.call-start = ((), (), s32[]{:S(2)}) async-start(), calls=%async_computation.8 | async-start | bytes 18874368 | tf_op jit(solution)/shard_map/all_gather | solution.py:80
  169.9 1.7 copy-start.6
  169.9 401.4 %all-gather.11.cloned.1.call-start = ((), (), s32[]{:S(2)}) async-start(), calls=%async_computation.9 | async-start | bytes 9437184 | tf_op jit(solution)/shard_map/all_gather | solution.py:81
  172.7 470.3 %all-reduce.9.cloned.1.call-start = ((), (), s32[]{:S(2)}) async-start(), calls=%async_computation.11 | async-start | bytes 4194304 | tf_op jit(solution)/shard_map/psum | solution.py:128
  593.2 89.0 %all-reduce.7.cloned.1.call-start = ((), (), s32[]{:S(2)}) async-start(), calls=%async_computation.10 | async-start | bytes 2097152 | tf_op jit(solution)/shard_map/psum | solution.py:117
  600.4 159.8 %all-reduce.11.cloned.1.call-start = ((), (), s32[]{:S(2)}) async-start(), calls=%async_computation.12 | async-start | bytes 4194304 | tf_op jit(solution)/shard_map/psum | solution.py:171
  682.3 5.3 copy-start.5
  686.3 1.3 copy-start
  690.8 2.4 copy-start.4
  690.8 3.8 copy-start.17
  690.8 4.7 copy-start.19
  708.2 120.3 %reduce-scatter.16.cloned.1.call-start = ((), (), s32[]{:S(2)}) async-start(), calls=%async_computation.17 | async-start | bytes 1179648
  763.8 156.0 %reduce-scatter.10.cloned.1.call-start = ((), (), s32[]{:S(2)}) async-start(), calls=%async_computation.14 | async-start | bytes 4718592 | tf_op jit(solution)/shard_map/reduce_scatter | solution.py:179
  768.2 362.7 %reduce-scatter.8.cloned.1.call-start = ((), (), s32[]{:S(2)}) async-start(), calls=%async_computation.13 | async-start | bytes 14155776 | tf_op jit(solution)/shard_map/reduce_scatter | solution.py:178
  776.6 637.3 %reduce-scatter.14.cloned.1.call-start = ((), (), s32[]{:S(2)}) async-start(), calls=%async_computation.16 | async-start | bytes 18874368 | tf_op jit(solution)/shard_map/reduce_scatter | solution.py:181
  786.4 1169.2 %reduce-scatter.12.cloned.1.call-start = ((), (), s32[]{:S(2)}) async-start(), calls=%async_computation.15 | async-start | bytes 37748736 | tf_op jit(solution)/shard_map/reduce_scatter | solution.py:180
  801.6 1.4 copy-start.9
  804.6 5.5 copy-start.14
  1416.7 544.0 %copy-start.1 = (f32[256,2048]{1,0:T(8,128)S(1)}, f32[256,2048]{1,0:T(8,128)}, u32[]{:S(2)}) copy-start(f32[256,2048]{1,0:T(8,128)} %copy-done) | copy-start | bytes 6291460
  2039.8 5.5 copy-start.22
  2039.8 5.5 copy-start.23
  2039.8 6.1 copy-start.12
  2039.8 6.1 copy-start.13
  2039.8 8.8 copy-start.8
  2045.3 3.3 copy-start.7
  (5 other events, 4.1 us)
Sparse Core Ops, SparseCore 0:
  10.8 101.4 all-gather.4
  115.0 47.3 all-gather.6
  166.1 49.9 all-reduce.4
  218.7 227.3 all-gather.8
  448.6 122.6 all-gather.10
  593.4 49.5 all-reduce.8
  645.9 36.3 all-reduce.6
  708.3 51.8 all-reduce.10
  764.2 64.2 reduce-scatter.15
  832.5 87.2 reduce-scatter.9
  923.4 207.4 reduce-scatter.7
  1134.6 279.2 reduce-scatter.13
  1417.7 537.7 reduce-scatter.11
where the time goes:
time: 2070 us; the launch traced here: 2060 us
  waiting for transfers between devices  1760 us (85%)
  matrix products  98 us (5%)
  local copies, waits for them, and re-layouts  62.6 us (3%)
  blocking collectives  62.2 us (3%)
  other arithmetic  60.2 us (3%)
    reduce_scatter x1, waiting for transfers between devices, on_device(): lax.psum_scatter(grad_lift, 'dp', scatter_dimension=1, tiled=True)  539 us
    reduce_scatter x1, waiting for transfers between devices, on_device(): lax.psum_scatter(grad_down, 'dp', scatter_dimension=0, tiled=True)  279 us
    all_gather x1, waiting for transfers between devices, on_device(): lax.all_gather(lift_weight.astype(bf16), 'dp', axis=1, tiled=True)  228 us
    reduce_scatter x1, waiting for transfers between devices, on_device(): lax.psum_scatter(grad_qkv, 'dp', scatter_dimension=1, tiled=True)  209 us
    all_gather x1, waiting for transfers between devices, on_device(): lax.all_gather(down_weight.astype(bf16), 'dp', axis=0, tiled=True)  115 us
    reduce_scatter x1, waiting for transfers between devices, on_device(): lax.psum_scatter(grad_out, 'dp', scatter_dimension=0, tiled=True)  89.1 us
    all_gather x1, waiting for transfers between devices, on_device(): lax.all_gather(qkv_weight.astype(bf16), 'dp', axis=1, tiled=True)  78.4 us
    unnamed x62, local copies, waits for them, and re-layouts  55.1 us
  transfers between devices with their start and end apart: 13, of which 13 were waited for; matrix products, arithmetic and copies ran while one was open for 5% of the time, Pallas kernels for 0%

commit v1 on v0

--- a/solution.py
+++ b/solution.py
@@ -3,6 +3,7 @@
 import jax.numpy as jnp
 from jax import lax
 from jax.sharding import PartitionSpec as P
+from jax.lax import all_gather
 
 HD = 128
 STEP = 10
@@ -125,9 +126,8 @@
     grad_up = (grad_hidden * gate * sigma).astype(bf16)
     grad_pair = jnp.stack([grad_gate, grad_up])
     grad_lift = jnp.einsum("td,ctf->cdf", normed_two, grad_pair, preferred_element_type=f32)
-    back_two = lax.psum(
-        jnp.einsum("ctf,cdf->td", grad_pair, w_lift, preferred_element_type=f32), "tensor"
-    )
+    mine = jnp.einsum("ctf,cdf->td", grad_pair, w_lift, preferred_element_type=f32)
+    back_two = jnp.sum(all_gather(mine, "tensor"), axis=0)
     grad_gain_two, grad_mid_norm = norm_backward(back_two, scaled_two, inverse_two, gain_two)
     grad_mid = grad_incoming + grad_mid_norm
     grad_branch = grad_mid.astype(bf16)

time: 2070 us -> 2070 us (level)
    all_gather x0 -> x1, waiting for transfers between devices: none -> 48.9 us  [on_device(): back_two = jnp.sum(all_gather(mine, 'tensor'), axis=0)]
    psum x1 -> x0, waiting for transfers between devices: 42 us -> none  [on_device(): lax.psum(jnp.einsum('ctf,cdf->td', grad_pair, w_lift, preferred_element_t...]
where the time goes in v1:
time: 2070 us
  waiting for transfers between devices  1760 us (85%)
  matrix products  98 us (5%)
  other arithmetic  65.9 us (3%)
  local copies, waits for them, and re-layouts  62.6 us (3%)
  blocking collectives  62.2 us (3%)
    reduce_scatter x1, waiting for transfers between devices, on_device(): lax.psum_scatter(grad_lift, 'dp', scatter_dimension=1, tiled=True)  538 us
    reduce_scatter x1, waiting for transfers between devices, on_device(): lax.psum_scatter(grad_down, 'dp', scatter_dimension=0, tiled=True)  282 us
    all_gather x1, waiting for transfers between devices, on_device(): lax.all_gather(lift_weight.astype(bf16), 'dp', axis=1, tiled=True)  228 us
    reduce_scatter x1, waiting for transfers between devices, on_device(): lax.psum_scatter(grad_qkv, 'dp', scatter_dimension=1, tiled=True)  208 us
    all_gather x1, waiting for transfers between devices, on_device(): lax.all_gather(down_weight.astype(bf16), 'dp', axis=0, tiled=True)  115 us
    reduce_scatter x1, waiting for transfers between devices, on_device(): lax.psum_scatter(grad_out, 'dp', scatter_dimension=0, tiled=True)  89.2 us
    all_gather x1, waiting for transfers between devices, on_device(): lax.all_gather(qkv_weight.astype(bf16), 'dp', axis=1, tiled=True)  78.4 us
    unnamed x62, local copies, waits for them, and re-layouts  55.1 us
  transfers between devices with their start and end apart: 13, of which 13 were waited for; matrix products, arithmetic and copies ran while one was open for 5% of the time, Pallas kernels for 0%

profile of v1, /device:TPU:0, one launch (start us, length us, event | category | flops | bytes accessed | tf_op | source)
XLA Modules:
  0.0 2069.6 jit_solution(2029839334260526096)
XLA Ops:
  10.7 22.7 %all_gather.21 = bf16[2,2048]{1,0:T(2,128)(2,1)S(1)} all-gather(bf16[2,256]{1,0:T(2,128)(2,1)S(1)} %convert_element_type.80), channel_id=1, replica_groups=mesh['dp'=8,'tensor'=4] {'dp'}, dimensions={1}, use_global_device_ids=true | all-gather | bytes 9216 | tf_op jit(solution)/shard_map/all_gather | solution.py:83
  33.8 78.4 %all-gather.7.cloned.1.call-done = bf16[3,2048,512]{2,1,0:T(8,128)(2,1)} async-done(((bf16[3,256,512]{2,1,0:T(8,128)(2,1)}), bf16[3,2048,512]{2,1,0:T(8,128)(2,1)}) %all-gather.7.cloned.1.call-update) | async-done | bytes 6291472 | tf_op jit(solution)/shard_map/all_gather | solution.py:79
  119.3 43.0 %all-gather.9.cloned.1.call-done = bf16[512,2048]{1,0:T(8,128)(2,1)} async-done(((bf16[64,2048]{1,0:T(8,128)(2,1)}), bf16[512,2048]{1,0:T(8,128)(2,1)}) %all-gather.9.cloned.1.call-update) | async-done | bytes 2097168 | tf_op jit(solution)/shard_map/all_gather | solution.py:80
  173.0 43.1 %all-reduce.4.cloned.1.call-done = f32[256,2048]{1,0:T(8,128)} async-done(((f32[256,2048]{1,0:T(8,128)}), f32[256,2048]{1,0:T(8,128)}) %all-reduce.4.cloned.1.call-update) | async-done | bytes 2097168 | tf_op jit(solution)/shard_map/psum | solution.py:110
  218.0 228.0 %all-gather.11.cloned.1.call-done = bf16[2,2048,2048]{2,1,0:T(8,128)(2,1)} async-done(((bf16[2,256,2048]{2,1,0:T(8,128)(2,1)}), bf16[2,2048,2048]{2,1,0:T(8,128)(2,1)}) %all-gather.11.cloned.1.call-update) | async-done | bytes 16777232 | tf_op jit(solution)/shard_map/all_gather | solution.py:81
  446.0 10.2 convolution_bitcast_fusion.2
  456.3 115.0 %all-gather.13.cloned.1.call-done = bf16[2048,2048]{1,0:T(8,128)(2,1)} async-done(((bf16[256,2048]{1,0:T(8,128)(2,1)}), bf16[2048,2048]{1,0:T(8,128)(2,1)}) %all-gather.13.cloned.1.call-update) | async-done | bytes 8388624 | tf_op jit(solution)/shard_map/all_gather | solution.py:82
  571.3 9.7 fusion.28
  580.9 12.3 convolution_bitcast_fusion.4
  593.3 7.0 convolution_convert_fusion
  600.9 48.9 %all-gather.15.cloned.1.call-done = f32[1024,2048]{1,0:T(8,128)} async-done(((f32[256,2048]{1,0:T(8,128)}), f32[1024,2048]{1,0:T(8,128)}) %all-gather.15.cloned.1.call-update) | async-done | bytes 8388624 | tf_op jit(solution)/shard_map/all_gather | solution.py:130
  649.8 5.7 reduce_sum.110
  657.7 31.4 %all-reduce.6.cloned.1.call-done = bf16[256,2048]{1,0:T(8,128)(2,1)} async-done(((bf16[256,2048]{1,0:T(8,128)(2,1)}), bf16[256,2048]{1,0:T(8,128)(2,1)}) %all-reduce.6.cloned.1.call-update) | async-done | bytes 1048592 | tf_op jit(solution)/shard_map/psum | solution.py:118
  708.8 6.2 convolution_bitcast_fusion.3
  715.0 52.0 %all-reduce.8.cloned.1.call-done = f32[256,2048]{1,0:T(8,128)} async-done(((f32[256,2048]{1,0:T(8,128)}), f32[256,2048]{1,0:T(8,128)}) %all-reduce.8.cloned.1.call-update) | async-done | bytes 2097168 | tf_op jit(solution)/shard_map/psum | solution.py:171
  775.1 9.6 fusion.54
  785.7 7.5 convolution_bitcast_fusion.1
  793.4 15.0 convolution_bitcast_fusion
  811.4 5.5 copy.83
  821.5 5.4 copy.80
  826.9 5.4 copy.81
  837.5 89.2 %reduce-scatter.10.cloned.1.call-done = f32[64,2048]{1,0:T(8,128)} async-done(((f32[512,2048]{1,0:T(8,128)}), f32[64,2048]{1,0:T(8,128)}) %reduce-scatter.10.cloned.1.call-update) | async-done | bytes 524304 | tf_op jit(solution)/shard_map/reduce_scatter | solution.py:179
  928.5 281.8 %reduce-scatter.14.cloned.1.call-done = f32[256,2048]{1,0:T(8,128)} async-done(((f32[2048,2048]{1,0:T(8,128)}), f32[256,2048]{1,0:T(8,128)}) %reduce-scatter.14.cloned.1.call-update) | async-done | bytes 2097168 | tf_op jit(solution)/shard_map/reduce_scatter | solution.py:181
  1213.1 207.7 %reduce-scatter.8.cloned.1.call-done = f32[3,256,512]{1,2,0:T(8,128)} async-done(((f32[3,2048,512]{1,2,0:T(8,128)}), f32[3,256,512]{1,2,0:T(8,128)}) %reduce-scatter.8.cloned.1.call-update) | async-done | bytes 1572880 | tf_op jit(solution)/shard_map/reduce_scatter | solution.py:178
  1424.5 538.1 %reduce-scatter.12.cloned.1.call-done = f32[2,256,2048]{1,2,0:T(8,128)} async-done(((f32[2,2048,2048]{1,2,0:T(8,128)}), f32[2,256,2048]{1,2,0:T(8,128)}) %reduce-scatter.12.cloned.1.call-update) | async-done | bytes 4194320 | tf_op jit(solution)/shard_map/reduce_scatter | solution.py:180
  1971.3 39.5 %psum.31 = f32[]{:T(128)} all-reduce(f32[]{:T(128)S(6)} %add.181), channel_id=1, replica_groups=mesh['dp'=8,'tensor'=4] {'dp','tensor'}, use_global_device_ids=true, to_apply=%region_20.21 | all-reduce | flops 1 | bytes 8 | tf_op jit(solution)/shard_map/psum | solution.py:191
  2011.5 5.7 multiply_subtract_fusion.2
  2020.2 11.3 multiply_subtract_fusion
  2031.6 5.3 copy.85
  2039.9 5.3 copy.87
  2046.9 5.5 copy.89
  2055.7 6.1 multiply_subtract_fusion.1
  (126 shorter events, 92.6 us)
Async XLA Ops:
  7.2 2.7 copy-start.11
  7.2 3.5 copy-start.20
  7.2 26.2 %copy-start.2 = (bf16[256,2048]{1,0:T(8,128)(2,1)S(1)}, bf16[256,2048]{1,0:T(8,128)(2,1)}, u32[]{:S(2)}) copy-start(bf16[256,2048]{1,0:T(8,128)(2,1)} %param.18) | copy-start | bytes 3145732
  7.2 26.5 %copy-start.21 = (s32[1,256]{1,0:T(1,128)S(1)}, s32[1,256]{1,0:T(1,128)}, u32[]{:S(2)}) copy-start(s32[1,256]{1,0:T(1,128)} %param.19) | copy-start | bytes 3076
  7.2 105.0 %all-gather.7.cloned.1.call-start = ((), (), s32[]{:S(2)}) async-start(), calls=%async_computation.5 | async-start | bytes 7077888 | tf_op jit(solution)/shard_map/all_gather | solution.py:79
  9.8 152.5 %all-gather.9.cloned.1.call-start = ((), (), s32[]{:S(2)}) async-start(), calls=%async_computation.6 | async-start | bytes 2359296 | tf_op jit(solution)/shard_map/all_gather | solution.py:80
  10.6 205.5 %all-reduce.4.cloned.1.call-start = ((), (), s32[]{:S(2)}) async-start(), calls=%async_computation.7 | async-start | bytes 4194304 | tf_op jit(solution)/shard_map/psum | solution.py:110
  166.0 280.1 %all-gather.11.cloned.1.call-start = ((), (), s32[]{:S(2)}) async-start(), calls=%async_computation.8 | async-start | bytes 18874368 | tf_op jit(solution)/shard_map/all_gather | solution.py:81
  169.9 1.7 copy-start.6
  169.9 401.4 %all-gather.13.cloned.1.call-start = ((), (), s32[]{:S(2)}) async-start(), calls=%async_computation.9 | async-start | bytes 9437184 | tf_op jit(solution)/shard_map/all_gather | solution.py:82
  172.7 477.2 %all-gather.15.cloned.1.call-start = ((), (), s32[]{:S(2)}) async-start(), calls=%async_computation.16 | async-start | bytes 10485760 | tf_op jit(solution)/shard_map/all_gather | solution.py:130
  593.2 95.9 %all-reduce.6.cloned.1.call-start = ((), (), s32[]{:S(2)}) async-start(), calls=%async_computation.10 | async-start | bytes 2097152 | tf_op jit(solution)/shard_map/psum | solution.py:118
  600.3 166.7 %all-reduce.8.cloned.1.call-start = ((), (), s32[]{:S(2)}) async-start(), calls=%async_computation.11 | async-start | bytes 4194304 | tf_op jit(solution)/shard_map/psum | solution.py:171
  689.1 5.3 copy-start.5
  693.1 1.3 copy-start
  697.7 2.4 copy-start.4
  697.7 3.8 copy-start.17
  697.7 4.7 copy-start.19
  715.0 120.3 %reduce-scatter.16.cloned.1.call-start = ((), (), s32[]{:S(2)}) async-start(), calls=%async_computation.17 | async-start | bytes 1179648
  770.6 156.1 %reduce-scatter.10.cloned.1.call-start = ((), (), s32[]{:S(2)}) async-start(), calls=%async_computation.13 | async-start | bytes 4718592 | tf_op jit(solution)/shard_map/reduce_scatter | solution.py:179
  775.0 435.3 %reduce-scatter.14.cloned.1.call-start = ((), (), s32[]{:S(2)}) async-start(), calls=%async_computation.15 | async-start | bytes 18874368 | tf_op jit(solution)/shard_map/reduce_scatter | solution.py:181
  784.8 636.1 %reduce-scatter.8.cloned.1.call-start = ((), (), s32[]{:S(2)}) async-start(), calls=%async_computation.12 | async-start | bytes 14155776 | tf_op jit(solution)/shard_map/reduce_scatter | solution.py:178
  793.2 1169.5 %reduce-scatter.12.cloned.1.call-start = ((), (), s32[]{:S(2)}) async-start(), calls=%async_computation.14 | async-start | bytes 37748736 | tf_op jit(solution)/shard_map/reduce_scatter | solution.py:180
  808.4 1.4 copy-start.9
  811.4 5.5 copy-start.14
  1424.5 543.3 %copy-start.1 = (f32[256,2048]{1,0:T(8,128)S(1)}, f32[256,2048]{1,0:T(8,128)}, u32[]{:S(2)}) copy-start(f32[256,2048]{1,0:T(8,128)} %copy-done) | copy-start | bytes 6291460
  2046.9 5.5 copy-start.22
  2046.9 5.5 copy-start.23
  2046.9 6.1 copy-start.12
  2046.9 6.1 copy-start.13
  2046.9 8.8 copy-start.8
  2052.4 3.3 copy-start.7
  (5 other events, 4.1 us)
Sparse Core Ops, SparseCore 0:
  10.8 101.4 all-gather.6
  115.0 47.3 all-gather.8
  166.1 49.9 all-reduce.3
  218.7 227.3 all-gather.10
  448.6 122.6 all-gather.12
  593.4 56.4 all-gather.14
  652.8 36.2 all-reduce.5
  715.1 51.8 all-reduce.7
  771.0 64.2 reduce-scatter.15
  839.3 87.3 reduce-scatter.9
  930.5 279.7 reduce-scatter.13
  1213.8 206.9 reduce-scatter.7
  1424.6 538.0 reduce-scatter.11
